TPU v7x, 128 devices: a whole 4x4x4 slice. The times are simulated.
128 devices in a mesh: dp: 16 (over x, y_lo, core), ctx: 8 (over y_hi, z).
Axes of the slice: x: 4, y: 4 (y_hi: 2, y_lo: 2; y = y_hi * 2 + y_lo), z: 4, core: 2. Of those that a mesh axis runs over, the one named last changes fastest.
Arguments:
- tokens: bfloat16 [16, 1792, 2048], P('dp', 'ctx'), may hold values from -6 to 6
- norm_gain: bfloat16 [2048], replicated, may hold values from 0.099609375 to 1.8984375
- q_weight: bfloat16 [2048, 2048], P('dp'), may hold values from -0.110927376 to 0.110927376
- k_weight: bfloat16 [2048, 2048], P('dp'), may hold values from -6.408155204503087 to 6.408155204503087
- v_weight: bfloat16 [2048, 2048], P('dp'), may hold values from -0.125 to 0.125
Outputs:
- attended: bfloat16 [16, 1792, 2048], P('dp', 'ctx')
All inputs are finite; a program needn't handle non-finite values.
Results may differ from a plain program's by a relative error of at most 0.0055.
The roundings to bfloat16 on the way count: a program that leaves them out, or rounds other values in their place, can miss the bound.
Values may be sent and summed in bfloat16 or wider, within the bound.
A program may use at most 128 MiB of HBM per device.

v0:
```python
import jax
import jax.numpy as jnp
from jax import lax
from jax.sharding import PartitionSpec as P

HEADS = 16
HEAD_DIM = 128


def rotate(values, positions):
    half = HEAD_DIM // 2
    shaped = values.reshape(values.shape[0], HEADS, HEAD_DIM)
    freqs = 10000.0 ** (-(jnp.arange(half).astype(jnp.float32) * 2.0) / HEAD_DIM)
    angles = positions[:, None] * freqs[None, :]
    cosine = jnp.cos(angles)[:, None, :]
    sine = jnp.sin(angles)[:, None, :]
    first = shaped[:, :, :half]
    second = shaped[:, :, half:]
    turned = jnp.concatenate(
        [first * cosine - second * sine, second * cosine + first * sine], axis=2
    )
    return turned.reshape(values.shape[0], HEADS * HEAD_DIM)


def shards(tokens, norm_gain, q_weight, k_weight, v_weight):
    seq_rows = tokens.shape[1]
    columns = q_weight.shape[1]
    own_block = lax.axis_index("ctx")
    rows = tokens[0].astype(jnp.float32)
    scale_rows = lax.rsqrt(jnp.mean(rows * rows, axis=1, keepdims=True) + 1e-05)
    normed = (rows * scale_rows * norm_gain.astype(jnp.float32)[None, :]).astype(jnp.bfloat16)
    pieces = (
        lax.all_gather(q_weight, "dp", axis=0, tiled=True),
        lax.all_gather(k_weight, "dp", axis=0, tiled=True),
        lax.all_gather(v_weight, "dp", axis=0, tiled=True),
    )
    count = pieces[0].shape[0]
    q_lin, k_lin, v_lin = tuple(
        (jnp.dot(normed, piece, preferred_element_type=jnp.float32) for piece in pieces)
    )
    values = v_lin.astype(jnp.bfloat16)
    own_positions = own_block * seq_rows + jnp.arange(seq_rows, dtype=jnp.int32)
    queries = rotate(q_lin, own_positions.astype(jnp.float32)).astype(jnp.bfloat16)
    keys = rotate(k_lin, own_positions.astype(jnp.float32)).astype(jnp.bfloat16)
    head_q = queries.reshape(seq_rows, HEADS, HEAD_DIM)
    factor = HEAD_DIM ** (-0.5)
    last_query = jnp.max(own_positions)
    start_state = (
        jnp.full((seq_rows, HEADS), -1e30, jnp.float32),
        jnp.zeros((seq_rows, HEADS), jnp.float32),
        jnp.zeros((seq_rows, HEADS, HEAD_DIM), jnp.float32),
    )
    key_block = lax.all_gather(keys, "ctx", axis=0, tiled=True)
    value_block = lax.all_gather(values, "ctx", axis=0, tiled=True)
    count = key_block.shape[0]
    key_pos = jnp.arange(count, dtype=jnp.int32)

    def work(state):
        peak, total, accum = state
        scores = (
            jnp.einsum(
                "qhd,khd->qhk",
                head_q,
                key_block.reshape(count, HEADS, HEAD_DIM),
                preferred_element_type=jnp.float32,
            )
            * factor
        )
        allowed = (key_pos[None, :] <= own_positions[:, None])[:, None, :]
        scores = jnp.where(allowed, scores, -1e30)
        new_peak = jnp.maximum(peak, jnp.max(scores, axis=2))
        expo = jnp.where(allowed, jnp.exp(scores - new_peak[:, :, None]), 0.0)
        total = jnp.sum(expo, axis=2)
        accum = jnp.einsum(
            "qhk,khd->qhd",
            expo.astype(jnp.bfloat16),
            value_block.reshape(count, HEADS, HEAD_DIM),
            preferred_element_type=jnp.float32,
        )
        return (new_peak, total, accum)

    peak, total, accum = lax.cond(
        jnp.int32(0) <= last_query, work, lambda state: state, start_state
    )
    attended = (accum / total[:, :, None]).reshape(seq_rows, columns).astype(jnp.bfloat16)
    return attended[None]


def solution(mesh):
    placed = (P("dp", "ctx", None), P(), P("dp", None), P("dp", None), P("dp", None))
    return jax.shard_map(
        shards, mesh=mesh, in_specs=placed, out_specs=P("dp", "ctx", None), check_vma=False
    )
```

profile of v0, /device:TPU:17, one launch (start us, length us, event | category | flops | bytes accessed | tf_op | source)
XLA Modules:
  0.0 417.8 jit_solution(14111547417479521798)
XLA Ops:
  6.5 0.0 all-gather.12.cloned.1.call-start
  6.5 0.7 all-gather.12.cloned.1.call-update
  7.3 0.0 all-gather.10.cloned.1.call-start
  7.3 0.7 all-gather.10.cloned.1.call-update
  8.0 0.0 all-gather.6.cloned.1.call-start
  8.1 0.7 all-gather.6.cloned.1.call-update
  8.7 0.0 all-gather.14.cloned.1.call-start
  8.8 0.7 convert_element_type.70
  9.5 1.4 fusion.21
  10.9 52.7 %all-gather.12.cloned.1.call-done = bf16[2048,2048]{1,0:T(8,128)(2,1)} async-done(((bf16[128,2048]{1,0:T(8,128)(2,1)}), bf16[2048,2048]{1,0:T(8,128)(2,1)}) %all-gather.12.cloned.1.call-update) | async-done | bytes 8388624 | tf_op jit(solution)/shard_map/all_gather | solution.py:35
  63.6 6.7 %convolution_convert_fusion = bf16[224,2048]{1,0:T(8,128)(2,1)} fusion(bf16[2048,2048]{1,0:T(8,128)(2,1)} %all-gather.12.cloned.1.call-done, bf16[1,224,2048]{2,1,0:T(8,128)(2,1)} %param.7, f32[2048]{0:T(1024)S(1)} %convert_element_type.70, f32[224]{0:T(256)S(1)} %add_rsqrt_fusion), kind=kOutput, calls=%fused_computation.18 | convolution fusion | flops 1881341952 | bytes 10232704 | tf_op jit(solution)/shard_map/dot_general | solution.py:39
  70.3 0.0 all-gather.14.cloned.1.call-update
  70.3 0.0 all-gather.8.cloned.1.call-start
  70.4 0.7 fusion.34
  71.1 0.5 multiply_cosine_fusion
  71.6 46.6 %all-gather.10.cloned.1.call-done = bf16[2048,2048]{1,0:T(8,128)(2,1)} async-done(((bf16[128,2048]{1,0:T(8,128)(2,1)}), bf16[2048,2048]{1,0:T(8,128)(2,1)}) %all-gather.10.cloned.1.call-update) | async-done | bytes 8388624 | tf_op jit(solution)/shard_map/all_gather | solution.py:33
  118.2 12.3 %copy.23 = bf16[2048,2048]{1,0:T(8,128)(2,1)} copy(bf16[2048,2048]{0,1:T(8,128)(2,1)} %bitcast.64) | data formatting | bytes 16777216 | tf_op jit(solution)/shard_map/dot_general | solution.py:39
  130.5 42.4 %all-gather.6.cloned.1.call-done = bf16[2048,2048]{1,0:T(8,128)(2,1)} async-done(((bf16[128,2048]{1,0:T(8,128)(2,1)}), bf16[2048,2048]{1,0:T(8,128)(2,1)}) %all-gather.6.cloned.1.call-update) | async-done | bytes 8388624 | tf_op jit(solution)/shard_map/all_gather | solution.py:34
  172.9 0.0 copy-start.1
  172.9 12.4 %copy.21 = bf16[2048,2048]{1,0:T(8,128)(2,1)} copy(bf16[2048,2048]{0,1:T(8,128)(2,1)} %bitcast.65) | data formatting | bytes 16777216 | tf_op jit(solution)/shard_map/dot_general | solution.py:39
  185.3 0.0 copy-done.1
  185.3 0.0 copy-start
  185.3 5.8 %fusion.30 = f32[224,16,128]{2,0,1:T(8,128)S(1)} fusion(bf16[16,128,2048]{2,1,0:T(8,128)(2,1)} %bitcast.66, bf16[1,224,2048]{2,1,0:T(8,128)(2,1)S(1)} %copy-done.1, f32[2048]{0:T(1024)S(1)} %convert_element_type.70, f32[224]{0:T(256)S(1)} %add_rsqrt_fusion), kind=kOutput, calls=%fused_computation.39 | convolution fusion | flops 1880883200 | bytes 11150208 | tf_op jit(solution)/shard_map/dot_general | solution.py:39
  191.1 0.8 copy-done
  191.9 2.8 fusion.32
  194.6 1.2 subtract_convert_fusion
  195.8 1.4 copy_bitcast_fusion
  197.2 0.0 all-gather.8.cloned.1.call-update
  197.9 0.5 pad_maximum_fusion
  198.5 71.5 %all-gather.14.cloned.1.call-done = bf16[1792,2048]{1,0:T(8,128)(2,1)} async-done(((bf16[224,2048]{1,0:T(8,128)(2,1)}), bf16[1792,2048]{1,0:T(8,128)(2,1)}) %all-gather.14.cloned.1.call-update) | async-done | bytes 7340048 | tf_op jit(solution)/shard_map/all_gather | solution.py:54
  270.0 97.4 %all-gather.8.cloned.1.call-done = bf16[1792,2048]{1,0:T(8,128)(2,1)} async-done(((bf16[224,2048]{1,0:T(8,128)(2,1)}), bf16[1792,2048]{1,0:T(8,128)(2,1)}) %all-gather.8.cloned.1.call-update) | async-done | bytes 7340048 | tf_op jit(solution)/shard_map/all_gather | solution.py:53
  367.4 41.7 %conditional.1 = (f32[224,16]{0,1:T(8,128)S(1)}, f32[224,16,128]{2,0,1:T(8,128)S(1)}) conditional(s32[]{:T(128)} %convert_element_type.66, () %tuple.13, (s32[1792]{0:T(1024)S(1)}, s32[224]{0:T(256)S(1)}, bf16[1792,2048]{1,0:T(8,128)(2,1)}, bf16[224,16,128]{2,0,1:T(8,128)(2,1)S(1)}, bf16[1792,2048]{1,0:T(8,128)(2,1)}) %tuple.14), branch_computations={%region_2.0_spmd, %region_3.6_spmd} | conditional | flops 3372225024 | bytes 96202640 | solution.py:82
  367.4 0.3 broadcast_compare_fusion
  367.7 13.3 %fusion = (f32[224,16]{0,1:T(8,128)S(1)}, f32[16,1792,224]{1,2,0:T(8,128)}) fusion(pred[224,1792]{1,0:T(8,128)(4,1)S(1)} %broadcast_compare_fusion, bf16[224,16,128]{2,0,1:T(8,128)(2,1)S(1)} %get-tuple-element.18, bf16[1792,2048]{1,0:T(8,128)(2,1)} %get-tuple-element.17), kind=kOutput, calls=%fused_computation.2 | convolution fusion | flops 1663431168 | bytes 34363392 | tf_op jit(solution)/shard_map/cond/branch_1_fun/qhd,khd->qhk/dot_general | solution.py:61
  381.0 14.4 %fusion.11 = f32[224,16,128]{2,0,1:T(8,128)S(1)} fusion(f32[16,1792,224]{1,2,0:T(8,128)} %get-tuple-element.25, f32[224,16]{0,1:T(8,128)S(1)} %broadcast_maximum_fusion, pred[224,1792]{1,0:T(8,128)(4,1)S(1)} %broadcast_compare_fusion, bf16[1792,2048]{1,0:T(8,128)(2,1)} %get-tuple-element.19), kind=kOutput, calls=%fused_computation.12 | convolution fusion | flops 1676279808 | bytes 35280896 | tf_op jit(solution)/shard_map/cond/branch_1_fun/qhk,khd->qhd/dot_general | solution.py:74
  395.4 13.6 %fusion.2 = f32[224,16]{0,1:T(8,128)S(1)} fusion(f32[16,1792,224]{1,2,0:T(8,128)} %get-tuple-element.25, f32[224,16]{0,1:T(8,128)S(1)} %broadcast_maximum_fusion, pred[224,1792]{1,0:T(8,128)(4,1)S(1)} %broadcast_compare_fusion), kind=kLoop, calls=%fused_computation.4 | loop fusion | flops 32109056 | bytes 26120192 | tf_op jit(solution)/shard_map/cond/branch_1_fun/reduce_sum | solution.py:73
  409.1 0.5 divide_convert_fusion
  409.6 0.4 copy.24
  410.0 1.3 convert_element_type.79
  (5 shorter events, 0.0 us)
Async XLA Ops:
  6.5 57.1 %all-gather.12.cloned.1.call-start = ((), (), s32[]{:S(2)}) async-start(), calls=%async_computation.3 | async-start | bytes 8912896 | tf_op jit(solution)/shard_map/all_gather | solution.py:35
  7.3 111.0 %all-gather.10.cloned.1.call-start = ((), (), s32[]{:S(2)}) async-start(), calls=%async_computation.2 | async-start | bytes 8912896 | tf_op jit(solution)/shard_map/all_gather | solution.py:33
  8.0 164.9 %all-gather.6.cloned.1.call-start = ((), (), s32[]{:S(2)}) async-start(), calls=%async_computation | async-start | bytes 8912896 | tf_op jit(solution)/shard_map/all_gather | solution.py:34
  8.7 261.2 %all-gather.14.cloned.1.call-start = ((), (), s32[]{:S(2)}) async-start(), calls=%async_computation.4 | async-start | bytes 8257536 | tf_op jit(solution)/shard_map/all_gather | solution.py:54
  70.3 297.0 %all-gather.8.cloned.1.call-start = ((), (), s32[]{:S(2)}) async-start(), calls=%async_computation.1 | async-start | bytes 8257536 | tf_op jit(solution)/shard_map/all_gather | solution.py:53
  172.9 12.4 %copy-start.1 = (bf16[1,224,2048]{2,1,0:T(8,128)(2,1)S(1)}, bf16[1,224,2048]{2,1,0:T(8,128)(2,1)}, u32[]{:S(2)}) copy-start(bf16[1,224,2048]{2,1,0:T(8,128)(2,1)} %param.7) | copy-start | bytes 2752516
  185.3 6.5 %copy-start = (bf16[2048,2048]{1,0:T(8,128)(2,1)S(1)}, bf16[2048,2048]{1,0:T(8,128)(2,1)}, u32[]{:S(2)}) copy-start(bf16[2048,2048]{1,0:T(8,128)(2,1)} %copy.21) | copy-start | bytes 25165828
Sparse Core Ops, SparseCore 0:
  9.0 54.5 all-gather.11
  65.3 52.8 all-gather.9
  120.0 52.9 all-gather.5
  175.1 94.8 all-gather.13
  272.1 95.2 all-gather.7
where the time goes:
time: 422 us; the launch traced here: 418 us
  waiting for transfers between devices  313 us (74%)
  matrix products  43 us (10%)
  local copies, waits for them, and re-layouts  27.2 us (6%)
  other arithmetic  20.9 us (5%)
  between operations  13.9 us (3%)
    all_gather x1, waiting for transfers between devices, shards(): key_block = lax.all_gather(keys, 'ctx', axis=0, tiled=True)  97.4 us
    all_gather x1, waiting for transfers between devices, shards(): value_block = lax.all_gather(values, 'ctx', axis=0, tiled=True)  71.5 us
    all_gather x1, waiting for transfers between devices, shards(): lax.all_gather(v_weight, 'dp', axis=0, tiled=True)  52.7 us
    all_gather x1, waiting for transfers between devices, shards(): lax.all_gather(q_weight, 'dp', axis=0, tiled=True)  46.6 us
    all_gather x1, waiting for transfers between devices, shards(): lax.all_gather(k_weight, 'dp', axis=0, tiled=True)  42.4 us
    dot_general x2, local copies, waits for them, and re-layouts, shards(): jnp.dot(normed, piece, preferred_element_type=jnp.float32)  24.7 us
    dot_general x3, matrix products, shards(): jnp.dot(normed, piece, preferred_element_type=jnp.float32)  15.2 us
    dot_general x1, matrix products, work(): jnp.einsum('qhk,khd->qhd', expo.astype(jnp.bfloat16), value_block.reshape...  14.4 us
  transfers between devices with their start and end apart: 5, of which 5 were waited for; matrix products, arithmetic and copies ran while one was open for 11% of the time, Pallas kernels for 0%

commit v1 on v0

v1 whole, which is shorter than its diff:
```python
import functools
import math

import jax
import jax.numpy as jnp
import numpy as np
from jax import lax
from jax.experimental import pallas as pl
from jax.experimental.pallas import tpu as pltpu
from jax.sharding import PartitionSpec as P

MESH = pl.DeviceIdType.MESH
HEADS = 16
HD = 128
D = 2048
ROWS = 224
LEN = 1792
WR = 128
WC = 256
HALF = ROWS // 2
QB = 256
NQ = LEN // QB
NCHUNK = 32
PB = 448


def tables():
    freqs = 10000.0 ** (-2.0 * np.arange(HD // 2) / HD)
    angles = np.arange(LEN)[:, None] * freqs[None, :]
    cosine, sine = np.cos(angles), np.sin(angles)
    return (
        np.concatenate([cosine, cosine], axis=1).astype(np.float32),
        np.concatenate([-sine, sine], axis=1).astype(np.float32),
    )


def kernel(
    tok, gain, qw, kw, vw, cos_hbm, sin_hbm, out,
    tbuf, nbuf, wbuf, qbuf, kbuf, vbuf, obuf, cosb, sinb,
    wrecv, wsend, trecv, tsend, precv, psend, osend, orecv, lsem,
):
    d, t = lax.axis_index("dp"), lax.axis_index("ctx")
    x, yl, c = d // 4, (d // 2) % 2, d % 2
    yh, z = t // 4, t % 4
    y = yh * 2 + yl
    home = c == yh
    away = c != yh

    def dev(x_, yl_, c_, yh_, z_):
        return (x_ * 4 + yl_ * 2 + c_, yh_ * 4 + z_)

    def chip_y(step, c_):
        y_ = (y + step) % 4
        return dev(x, y_ % 2, c_, y_ // 2, z)

    partner = dev(x, yl, 1 - c, yh, z)
    pair = dev(x, yl, 1 - c, 1 - yh, z)
    xp, xm = dev((x + 1) % 4, yl, c, yh, z), dev((x + 3) % 4, yl, c, yh, z)
    zp, zm = dev(x, yl, c, yh, (z + 1) % 4), dev(x, yl, c, yh, (z + 3) % 4)

    def send(src, dst, ss, rs, to):
        return pltpu.make_async_remote_copy(
            src_ref=src, dst_ref=dst, send_sem=ss, recv_sem=rs, device_id=to, device_id_type=MESH
        )

    def wslot(e):
        return wbuf.at[:, pl.ds(pl.multiple_of(e * WR, WR), WR), :]

    def wslot_one(i, e):
        return wbuf.at[i, pl.ds(pl.multiple_of(e * WR, WR), WR), :]

    def wcols(ref, c_):
        return ref.at[:, pl.ds(pl.multiple_of(z * 512 + c_ * WC, WC), WC)]

    def tslot(z_, h):
        return tbuf.at[c * 4 + z_, pl.ds(h * HALF, HALF), :]

    weights = (qw, kw, vw)
    for i, w in enumerate(weights):
        pltpu.make_async_copy(wcols(w, c), wslot_one(i, d), wrecv.at[0, 0]).start()

    @pl.when(home)
    def _():
        for h in range(2):
            pltpu.make_async_copy(tok.at[pl.ds(h * HALF, HALF), :], tslot(z, h), trecv.at[0, h]).start()

    pltpu.make_async_copy(cos_hbm, cosb, lsem.at[0]).start()
    pltpu.make_async_copy(sin_hbm, sinb, lsem.at[1]).start()

    barrier = pltpu.get_barrier_semaphore()

    def greet(to):
        pl.semaphore_signal(barrier, inc=1, device_id=to, device_id_type=MESH)

    for k in range(1, 16):
        j = (c * 8 + t + k) % 16
        greet((x * 4 + yl * 2 + j // 8, j % 8))
    greet(xp)
    greet(xm)
    for step in (1, 3):
        for c_ in range(2):
            greet(chip_y(step, c_))
    pl.semaphore_wait(barrier, 21)

    for i, w in enumerate(weights):
        send(wcols(w, c), wslot_one(i, d), wsend.at[0, 0], wrecv.at[0, 2], chip_y(1, c)).start()
        send(wcols(w, 1 - c), wslot_one(i, d), wsend.at[0, 1], wrecv.at[0, 3], chip_y(3, 1 - c)).start()
        send(wcols(w, 1 - c), wslot_one(i, d), wsend.at[0, 2], wrecv.at[0, 1], partner).start()

    def exchange(h):
        there = tbuf.at[(1 - c) * 4 + z, pl.ds(h * HALF, HALF), :]
        return send(tok.at[pl.ds(h * HALF, HALF), :], there, tsend.at[0, h], trecv.at[0, h], pair)

    @pl.when(away)
    def _():
        exchange(0).start()
        exchange(1).start()

    own = [d, x * 4 + yl * 2 + (1 - c), x * 4 + (1 - yl) * 2 + c, x * 4 + (1 - yl) * 2 + (1 - c)]

    def shift(e, s):
        return (e + 4 * s) % 16

    def wait_w(g, k, e):
        send(wslot(e), wslot(e), wsend.at[0, 0], wrecv.at[g, k], partner).wait_recv()

    def wait_w_local():
        for i, w in enumerate(weights):
            pltpu.make_async_copy(wcols(w, c), wslot_one(i, d), wrecv.at[0, 0]).wait()

    def x_first(k):
        e = own[k]
        return (
            send(wslot(e), wslot(e), wsend.at[1, k], wrecv.at[1, k], xp),
            send(wslot(e), wslot(e), wsend.at[2, k], wrecv.at[2, k], xm),
        )

    def x_second(k):
        if k % 2 == 0:
            e = shift(own[k], 3)
            return send(wslot(e), wslot(e), wsend.at[3, k], wrecv.at[3, k], xp)
        e = shift(own[k], 1)
        return send(wslot(e), wslot(e), wsend.at[3, k], wrecv.at[3, k], xm)

    def z_first(h):
        return (
            send(tslot(z, h), tslot(z, h), tsend.at[1, h], trecv.at[1, h], zp),
            send(tslot(z, h), tslot(z, h), tsend.at[2, h], trecv.at[2, h], zm),
        )

    def z_second(h):
        z_ = (z + (3, 1)[h]) % 4
        return send(tslot(z_, h), tslot(z_, h), tsend.at[3, h], trecv.at[3, h], (zp, zm)[h])

    zs = [z, (z + 3) % 4, (z + 1) % 4, (z + 2) % 4]

    def to_partner(g, h):
        return send(tslot(zs[g], h), tslot(zs[g], h), psend.at[g, h], precv.at[g, h], partner)

    def wait_t(g, h):
        send(tslot(zs[g], h), tslot(zs[g], h), tsend.at[1, h], trecv.at[g, h], partner).wait_recv()

    def wait_own_t(h):
        @pl.when(home)
        def _():
            pltpu.make_async_copy(tok.at[pl.ds(h * HALF, HALF), :], tslot(z, h), trecv.at[0, h]).wait()

        @pl.when(away)
        def _():
            wait_t(0, h)

    def start_both(pair_):
        pair_[0].start()
        pair_[1].start()

    wait_w_local()
    start_both(x_first(0))

    @pl.when(home)
    def _():
        for h in range(2):
            wait_own_t(h)
            start_both(z_first(h))
            to_partner(0, h).start()

    for k in range(1, 4):
        wait_w(0, k, own[k])
        start_both(x_first(k))

    @pl.when(away)
    def _():
        for h in range(2):
            wait_own_t(h)
            start_both(z_first(h))
            to_partner(0, h).start()

    wait_w(1, 0, shift(own[0], 3))
    x_second(0).start()
    wait_w(2, 1, shift(own[1], 1))
    x_second(1).start()
    wait_t(1, 0)
    z_second(0).start()
    to_partner(1, 0).start()
    wait_t(2, 1)
    z_second(1).start()
    to_partner(2, 1).start()
    wait_w(1, 2, shift(own[2], 3))
    x_second(2).start()
    wait_w(2, 3, shift(own[3], 1))
    x_second(3).start()
    wait_t(1, 1)
    to_partner(1, 1).start()
    wait_t(2, 0)
    to_partner(2, 0).start()
    wait_t(3, 0)
    to_partner(3, 0).start()
    wait_t(3, 1)
    to_partner(3, 1).start()
    for k in (1, 3):
        wait_w(1, k, shift(own[k], 3))
    for k in (0, 2):
        wait_w(2, k, shift(own[k], 1))
    for k in range(4):
        wait_w(3, k, shift(own[k], 2))

    def pslot(z_, h):
        return tbuf.at[(1 - c) * 4 + z_, pl.ds(h * HALF, HALF), :]

    for g in range(4):
        for h in range(2):
            send(pslot(zs[g], h), pslot(zs[g], h), psend.at[g, h], precv.at[g, h], partner).wait_recv()
    pltpu.make_async_copy(cos_hbm, cosb, lsem.at[0]).wait()
    pltpu.make_async_copy(sin_hbm, sinb, lsem.at[1]).wait()

    gain_row = gain[...].astype(jnp.float32)

    def norm_rows(i, carry):
        block, part = i // (ROWS // NCHUNK), i % (ROWS // NCHUNK)
        rows = tbuf[block, pl.ds(pl.multiple_of(part * NCHUNK, NCHUNK), NCHUNK), :].astype(jnp.float32)
        scale = lax.rsqrt(jnp.mean(rows * rows, axis=1, keepdims=True) + 1e-05)
        nbuf[pl.ds(pl.multiple_of(i * NCHUNK, NCHUNK), NCHUNK), :] = (rows * scale * gain_row).astype(jnp.bfloat16)
        return carry

    lax.fori_loop(0, LEN // NCHUNK, norm_rows, 0)

    def turned(lin, rows):
        cosine, sine = cosb[rows, :], sinb[rows, :]
        parts = []
        for h in range(2):
            v = lin[:, h * HD : (h + 1) * HD]
            parts.append((v * cosine + pltpu.roll(v, HD // 2, 1) * sine).astype(jnp.bfloat16))
        return parts

    def project(i, carry):
        rows = pl.ds(pl.multiple_of(i * PB, PB), PB)
        block = nbuf[rows, :]
        q = jnp.dot(block, wbuf[0], preferred_element_type=jnp.float32)
        for h, part in enumerate(turned(q, rows)):
            qbuf[h, rows, :] = part
        k = jnp.dot(block, wbuf[1], preferred_element_type=jnp.float32)
        for h, part in enumerate(turned(k, rows)):
            kbuf[h, rows, :] = part
        v = jnp.dot(block, wbuf[2], preferred_element_type=jnp.float32).astype(jnp.bfloat16)
        for h in range(2):
            vbuf[h, rows, :] = v[:, h * HD : (h + 1) * HD]
        return carry

    lax.fori_loop(0, LEN // PB, project, 0)

    factor = HD ** (-0.5) * math.log2(math.e)
    nt = (((1,), (1,)), ((), ()))
    rows_i = lax.broadcasted_iota(jnp.int32, (QB, QB), 0)
    cols_i = lax.broadcasted_iota(jnp.int32, (QB, QB), 1)
    allowed = cols_i <= rows_i
    mycols = pl.ds(pl.multiple_of(z * 512 + c * WC, WC), WC)

    def to_owner(b):
        return send(
            obuf.at[pl.ds(b * ROWS, ROWS), :], out.at[:, mycols], osend.at[b], orecv.at[z * 2 + c],
            dev(x, yl, yh, b // 4, b % 4),
        )

    def to_self(b):
        return pltpu.make_async_copy(obuf.at[pl.ds(b * ROWS, ROWS), :], out.at[:, mycols], osend.at[b])

    def own_block(b):
        return jnp.logical_and(home, t == b)

    sent = 0
    for j in range(NQ):

        def one_head(h, carry, j=j):
            q = qbuf[h, pl.ds(j * QB, QB), :]
            s_d = lax.dot_general(q, kbuf[h, pl.ds(j * QB, QB), :], nt, preferred_element_type=jnp.float32)
            s_d = jnp.where(allowed, s_d, -1e30)
            top = jnp.max(s_d, axis=1, keepdims=True)
            if j:
                s_p = lax.dot_general(q, kbuf[h, pl.ds(0, j * QB), :], nt, preferred_element_type=jnp.float32)
                top = jnp.maximum(top, jnp.max(s_p, axis=1, keepdims=True))
            e_d = jnp.exp2((s_d - top) * factor)
            total = jnp.sum(e_d, axis=1, keepdims=True)
            acc = jnp.dot(e_d.astype(jnp.bfloat16), vbuf[h, pl.ds(j * QB, QB), :], preferred_element_type=jnp.float32)
            if j:
                e_p = jnp.exp2((s_p - top) * factor)
                total = total + jnp.sum(e_p, axis=1, keepdims=True)
                acc = acc + jnp.dot(
                    e_p.astype(jnp.bfloat16), vbuf[h, pl.ds(0, j * QB), :], preferred_element_type=jnp.float32
                )
            obuf[pl.ds(j * QB, QB), pl.ds(pl.multiple_of(h * HD, HD), HD)] = (acc / total).astype(jnp.bfloat16)
            return carry

        lax.fori_loop(0, 2, one_head, 0)
        while sent < 8 and (sent + 1) * ROWS <= (j + 1) * QB:

            @pl.when(own_block(sent))
            def _(b=sent):
                to_self(b).start()

            @pl.when(jnp.logical_not(own_block(sent)))
            def _(b=sent):
                to_owner(b).start()

            sent += 1

    for z_ in range(4):
        for c_ in range(2):
            cols = pl.ds((z_ * 2 + c_) * WC, WC)
            mine = jnp.logical_and(home, jnp.logical_and(z == z_, c == c_))

            @pl.when(jnp.logical_not(mine))
            def _(i=z_ * 2 + c_, cols=cols):
                send(obuf.at[pl.ds(0, ROWS), :], out.at[:, cols], osend.at[0], orecv.at[i], partner).wait_recv()

    for b in range(8):

        @pl.when(own_block(b))
        def _(b=b):
            to_self(b).wait()

        @pl.when(jnp.logical_not(own_block(b)))
        def _(b=b):
            to_owner(b).wait_send()

    for i in range(3):
        send(wslot(d), wslot(d), wsend.at[0, i], wrecv.at[0, 0], partner).wait_send()
    for k in range(4):
        for copy in x_first(k):
            copy.wait_send()
        x_second(k).wait_send()
    for h in range(2):

        @pl.when(away)
        def _(h=h):
            exchange(h).wait_send()

        for copy in z_first(h):
            copy.wait_send()
        z_second(h).wait_send()
        for g in range(4):
            to_partner(g, h).wait_send()


def shards(tokens, norm_gain, q_weight, k_weight, v_weight):
    cosine, sine = tables()
    anywhere = pl.BlockSpec(memory_space=pl.ANY)
    bf, dma = jnp.bfloat16, pltpu.SemaphoreType.DMA
    attended = pl.pallas_call(
        kernel,
        out_shape=jax.ShapeDtypeStruct((ROWS, D), bf),
        in_specs=[anywhere, pl.BlockSpec(memory_space=pltpu.VMEM)] + [anywhere] * 5,
        out_specs=anywhere,
        scratch_shapes=[
            pltpu.VMEM((8, ROWS, D), bf),
            pltpu.VMEM((LEN, D), bf),
            pltpu.VMEM((3, D, WC), bf),
            pltpu.VMEM((2, LEN, HD), bf),
            pltpu.VMEM((2, LEN, HD), bf),
            pltpu.VMEM((2, LEN, HD), bf),
            pltpu.VMEM((LEN, WC), bf),
            pltpu.VMEM((LEN, HD), jnp.float32),
            pltpu.VMEM((LEN, HD), jnp.float32),
            dma((4, 4)),
            dma((4, 4)),
            dma((4, 2)),
            dma((4, 2)),
            dma((4, 2)),
            dma((4, 2)),
            dma((8,)),
            dma((8,)),
            dma((2,)),
        ],
        compiler_params=pltpu.CompilerParams(
            collective_id=0, has_side_effects=True, vmem_limit_bytes=60 * 2**20
        ),
        name="attention_block",
    )(tokens[0], norm_gain[None, :], q_weight, k_weight, v_weight, jnp.asarray(cosine), jnp.asarray(sine))
    return attended[None]


def solution(mesh):
    placed = (P("dp", "ctx", None), P(), P("dp", None), P("dp", None), P("dp", None))
    return jax.shard_map(
        shards, mesh=mesh, in_specs=placed, out_specs=P("dp", "ctx", None), check_vma=False
    )
```

time: 422 us -> 81.6 us (0.19)
  waiting for transfers between devices: 313 us -> 0 us
  Pallas kernels: 0 us -> 77.9 us
  matrix products: 43 us -> 0 us
  local copies, waits for them, and re-layouts: 27.2 us -> 3.49 us
  other arithmetic: 20.9 us -> 0 us
  between operations: 13.9 us -> 0.01 us
    all_gather x5 -> x0, waiting for transfers between devices: 311 us -> none  [the longest x1 97.4 us: shards(): key_block = lax.all_gather(keys, 'ctx', axis=0, tiled=True)]
    pallas_call x0 -> x1, Pallas kernels: none -> 77.9 us  [shards(): pl.pallas_call(kernel, out_shape=jax.ShapeDtypeStruct((ROWS, D), bf), in_...]
    dot_general x5 -> x0, matrix products: 43 us -> none  [the longest x3 15.2 us: shards(): jnp.dot(normed, piece, preferred_element_type=jnp.float32)]
    dot_general x2 -> x0, local copies, waits for them, and re-layouts: 24.7 us -> none  [shards(): jnp.dot(normed, piece, preferred_element_type=jnp.float32)]
    reduce_sum x2 -> x0, other arithmetic: 15.1 us -> none  [the longest x1 13.6 us: work(): total = jnp.sum(expo, axis=2)]
  transfers between devices with their start and end apart: 5 -> 0, of which waited for: 5 -> 0; matrix products, arithmetic and copies ran while one was open for 11% -> 0% of each run, Pallas kernels for 0% -> 0%
where the time goes in v1:
time: 81.6 us; the launch traced here: 81.4 us
  Pallas kernels  77.9 us (95%)
  local copies, waits for them, and re-layouts  3.49 us (4%)
    pallas_call x1, Pallas kernels, shards(): pl.pallas_call(kernel, out_shape=jax.ShapeDtypeStruct((ROWS, D), bf), in_...  77.9 us
    unnamed x1, local copies, waits for them, and re-layouts  2.2 us

profile of v1, /device:TPU:17, one launch (start us, length us, event | category | flops | bytes accessed | tf_op | source)
XLA Modules:
  0.0 81.4 jit_solution(2012186433557531030)
XLA Ops:
  0.0 1.3 %broadcast_in_dim.6.gain = bf16[1,2048]{1,0:T(2,128)(2,1)} reshape(bf16[2048]{0:T(1024)(128)(2,1)} %param.8) | data formatting | bytes 8192 | tf_op jit(solution)/shard_map/broadcast_in_dim | solution.py:396
  1.3 77.9 %attention_block.1 = bf16[224,2048]{1,0:T(8,128)(2,1)} custom-call(bf16[224,2048]{1,0:T(8,128)(2,1)} %bitcast.3, bf16[1,2048]{1,0:T(2,128)(2,1)} %broadcast_in_dim.6.gain, bf16[128,2048]{1,0:T(8,128)(2,1)} %qw.1, bf16[128,2048]{1,0:T(8,128)(2,1)} %kw.1, bf16[128,2048]{1,0:T(8,128)(2,1)} %vw.1, f32[1792,128]{1,0:T(8,128)} %constant.4.clone.cos_hbm, ...), custom_call_target="tpu_custom_call" | custom-call | tf_op jit(solution)/shard_map/attention_block/pallas_call | solution.py:367
  79.2 2.2 %copy.9 = bf16[1,224,2048]{2,1,0:T(8,128)(2,1)} copy(bf16[1,224,2048]{2,1,0:T(8,128)(2,1)} %bitcast.2) | data formatting | bytes 1835008

commit v2 on v1

--- a/solution.py
+++ b/solution.py
@@ -21,7 +21,6 @@
 QB = 256
 NQ = LEN // QB
 NCHUNK = 32
-PB = 448
 
 
 def tables():
@@ -173,75 +172,52 @@
         pair_[0].start()
         pair_[1].start()
 
-    wait_w_local()
-    start_both(x_first(0))
-
-    @pl.when(home)
-    def _():
-        for h in range(2):
-            wait_own_t(h)
-            start_both(z_first(h))
-            to_partner(0, h).start()
-
-    for k in range(1, 4):
-        wait_w(0, k, own[k])
+    def x_start(k):
+        if k == 0:
+            wait_w_local()
+        else:
+            wait_w(0, k, own[k])
         start_both(x_first(k))
 
-    @pl.when(away)
-    def _():
-        for h in range(2):
-            wait_own_t(h)
-            start_both(z_first(h))
-            to_partner(0, h).start()
-
-    wait_w(1, 0, shift(own[0], 3))
-    x_second(0).start()
-    wait_w(2, 1, shift(own[1], 1))
-    x_second(1).start()
-    wait_t(1, 0)
-    z_second(0).start()
-    to_partner(1, 0).start()
-    wait_t(2, 1)
-    z_second(1).start()
-    to_partner(2, 1).start()
-    wait_w(1, 2, shift(own[2], 3))
-    x_second(2).start()
-    wait_w(2, 3, shift(own[3], 1))
-    x_second(3).start()
-    wait_t(1, 1)
-    to_partner(1, 1).start()
-    wait_t(2, 0)
-    to_partner(2, 0).start()
-    wait_t(3, 0)
-    to_partner(3, 0).start()
-    wait_t(3, 1)
-    to_partner(3, 1).start()
-    for k in (1, 3):
-        wait_w(1, k, shift(own[k], 3))
-    for k in (0, 2):
-        wait_w(2, k, shift(own[k], 1))
-    for k in range(4):
-        wait_w(3, k, shift(own[k], 2))
-
-    def pslot(z_, h):
-        return tbuf.at[(1 - c) * 4 + z_, pl.ds(h * HALF, HALF), :]
-
-    for g in range(4):
-        for h in range(2):
-            send(pslot(zs[g], h), pslot(zs[g], h), psend.at[g, h], precv.at[g, h], partner).wait_recv()
-    pltpu.make_async_copy(cos_hbm, cosb, lsem.at[0]).wait()
-    pltpu.make_async_copy(sin_hbm, sinb, lsem.at[1]).wait()
-
-    gain_row = gain[...].astype(jnp.float32)
-
-    def norm_rows(i, carry):
-        block, part = i // (ROWS // NCHUNK), i % (ROWS // NCHUNK)
-        rows = tbuf[block, pl.ds(pl.multiple_of(part * NCHUNK, NCHUNK), NCHUNK), :].astype(jnp.float32)
-        scale = lax.rsqrt(jnp.mean(rows * rows, axis=1, keepdims=True) + 1e-05)
-        nbuf[pl.ds(pl.multiple_of(i * NCHUNK, NCHUNK), NCHUNK), :] = (rows * scale * gain_row).astype(jnp.bfloat16)
-        return carry
-
-    lax.fori_loop(0, LEN // NCHUNK, norm_rows, 0)
+    def x_forward(k):
+        if k % 2 == 0:
+            wait_w(1, k, shift(own[k], 3))
+        else:
+            wait_w(2, k, shift(own[k], 1))
+        x_second(k).start()
+
+    def duty(role, g, h):
+        @pl.when(role)
+        def _():
+            if g == 0:
+                wait_own_t(h)
+                start_both(z_first(h))
+            else:
+                wait_t(g, h)
+                if (g, h) in ((1, 0), (2, 1)):
+                    z_second(h).start()
+            to_partner(g, h).start()
+
+    def ready(role, g):
+        @pl.when(role)
+        def _():
+            for h in range(2):
+                there = tbuf.at[(1 - c) * 4 + zs[g], pl.ds(h * HALF, HALF), :]
+                send(there, there, psend.at[g, h], precv.at[g, h], partner).wait_recv()
+
+    gain_row = gain[...].astype(jnp.float32).reshape(1, D)
+
+    def norm(plane, g):
+        block = plane * 4 + zs[g]
+
+        def norm_rows(i, carry):
+            rows = tbuf[block, pl.ds(pl.multiple_of(i * NCHUNK, NCHUNK), NCHUNK), :].astype(jnp.float32)
+            scale = lax.rsqrt(jnp.mean(rows * rows, axis=1, keepdims=True) + 1e-05)
+            to = pl.ds(pl.multiple_of(block * ROWS + i * NCHUNK, NCHUNK), NCHUNK)
+            nbuf[to, :] = (rows * scale * gain_row).astype(jnp.bfloat16)
+            return carry
+
+        lax.fori_loop(0, ROWS // NCHUNK, norm_rows, 0)
 
     def turned(lin, rows):
         cosine, sine = cosb[rows, :], sinb[rows, :]
@@ -251,8 +227,8 @@
             parts.append((v * cosine + pltpu.roll(v, HD // 2, 1) * sine).astype(jnp.bfloat16))
         return parts
 
-    def project(i, carry):
-        rows = pl.ds(pl.multiple_of(i * PB, PB), PB)
+    def project(first):
+        rows = pl.ds(pl.multiple_of(first * ROWS, ROWS), ROWS)
         block = nbuf[rows, :]
         q = jnp.dot(block, wbuf[0], preferred_element_type=jnp.float32)
         for h, part in enumerate(turned(q, rows)):
@@ -263,9 +239,68 @@
         v = jnp.dot(block, wbuf[2], preferred_element_type=jnp.float32).astype(jnp.bfloat16)
         for h in range(2):
             vbuf[h, rows, :] = v[:, h * HD : (h + 1) * HD]
-        return carry
-
-    lax.fori_loop(0, LEN // PB, project, 0)
+
+    def project_some(plane, groups):
+        lo, hi = groups
+
+        def one(g, carry):
+            z_ = lax.rem(z + jnp.where(g == 0, 0, jnp.where(g == 1, 3, jnp.where(g == 2, 1, 2))), 4)
+            project(plane * 4 + z_)
+            return carry
+
+        lax.fori_loop(lo, hi, one, 0)
+
+    x_start(0)
+    duty(home, 0, 0)
+    duty(home, 0, 1)
+    x_start(1)
+    ready(away, 0)
+    norm(yh, 0)
+    x_start(2)
+    x_start(3)
+    duty(away, 0, 0)
+    x_forward(0)
+    duty(home, 1, 0)
+    x_forward(1)
+    duty(home, 2, 1)
+    duty(home, 1, 1)
+    duty(home, 2, 0)
+    duty(away, 0, 1)
+    ready(away, 1)
+    norm(yh, 1)
+    x_forward(2)
+    ready(away, 2)
+    norm(yh, 2)
+    x_forward(3)
+    duty(home, 3, 0)
+    duty(home, 3, 1)
+    ready(home, 0)
+    norm(1 - yh, 0)
+    ready(away, 3)
+    norm(yh, 3)
+    duty(away, 1, 0)
+    duty(away, 2, 1)
+    duty(away, 1, 1)
+    duty(away, 2, 0)
+    ready(home, 1)
+    norm(1 - yh, 1)
+    ready(home, 2)
+    norm(1 - yh, 2)
+    for k in (1, 3):
+        wait_w(1, k, shift(own[k], 3))
+    for k in (0, 2):
+        wait_w(2, k, shift(own[k], 1))
+    for k in range(4):
+        wait_w(3, k, shift(own[k], 2))
+    pltpu.make_async_copy(cos_hbm, cosb, lsem.at[0]).wait()
+    pltpu.make_async_copy(sin_hbm, sinb, lsem.at[1]).wait()
+    project_some(yh, (0, 4))
+    duty(away, 3, 0)
+    duty(away, 3, 1)
+    project_some(1 - yh, (0, 3))
+    ready(home, 3)
+    norm(1 - yh, 3)
+    project_some(1 - yh, (3, 4))
 
     factor = HD ** (-0.5) * math.log2(math.e)
     nt = (((1,), (1,)), ((), ()))
@@ -393,7 +428,7 @@
             collective_id=0, has_side_effects=True, vmem_limit_bytes=60 * 2**20
         ),
         name="attention_block",
-    )(tokens[0], norm_gain[None, :], q_weight, k_weight, v_weight, jnp.asarray(cosine), jnp.asarray(sine))
+    )(tokens[0], norm_gain, q_weight, k_weight, v_weight, jnp.asarray(cosine), jnp.asarray(sine))
     return attended[None]
 
 

time: 81.6 us -> 70.4 us (0.86)
  the two profiles are of different devices: /device:TPU:17 before, /device:TPU:112 now
where the time goes in v2:
time: 70.4 us; the launch traced here: 70.3 us
  Pallas kernels  68.1 us (97%)
  local copies, waits for them, and re-layouts  2.2 us (3%)
    pallas_call x1, Pallas kernels, shards(): pl.pallas_call(kernel, out_shape=jax.ShapeDtypeStruct((ROWS, D), bf), in_...  68.1 us
    unnamed x1, local copies, waits for them, and re-layouts  2.2 us

profile of v2, /device:TPU:112, one launch (start us, length us, event | category | flops | bytes accessed | tf_op | source)
XLA Modules:
  0.0 70.3 jit_solution(8477940372523469363)
XLA Ops:
  0.0 68.1 %attention_block.1 = bf16[224,2048]{1,0:T(8,128)(2,1)} custom-call(bf16[224,2048]{1,0:T(8,128)(2,1)} %bitcast.3, bf16[2048]{0:T(1024)(128)(2,1)} %gain.1, bf16[128,2048]{1,0:T(8,128)(2,1)} %qw.1, bf16[128,2048]{1,0:T(8,128)(2,1)} %kw.1, bf16[128,2048]{1,0:T(8,128)(2,1)} %vw.1, f32[1792,128]{1,0:T(8,128)} %constant.4.clone.cos_hbm, ...), custom_call_target="tpu_custom_call" | custom-call | tf_op jit(solution)/shard_map/attention_block/pallas_call | solution.py:402
  68.1 2.2 %copy.9 = bf16[1,224,2048]{2,1,0:T(8,128)(2,1)} copy(bf16[1,224,2048]{2,1,0:T(8,128)(2,1)} %bitcast.2) | data formatting | bytes 1835008

commit v3 on v2

--- a/solution.py
+++ b/solution.py
@@ -20,7 +20,7 @@
 HALF = ROWS // 2
 QB = 256
 NQ = LEN // QB
-NCHUNK = 32
+NCHUNK = 16
 
 
 def tables():
@@ -36,7 +36,7 @@
 def kernel(
     tok, gain, qw, kw, vw, cos_hbm, sin_hbm, out,
     tbuf, nbuf, wbuf, qbuf, kbuf, vbuf, obuf, cosb, sinb,
-    wrecv, wsend, trecv, tsend, precv, psend, osend, orecv, lsem,
+    yrecv, ysend, wrecv, wsend, trecv, tsend, precv, psend, osend, orecv, lsem,
 ):
     d, t = lax.axis_index("dp"), lax.axis_index("ctx")
     x, yl, c = d // 4, (d // 2) % 2, d % 2
@@ -91,19 +91,15 @@
     def greet(to):
         pl.semaphore_signal(barrier, inc=1, device_id=to, device_id_type=MESH)
 
-    for k in range(1, 16):
-        j = (c * 8 + t + k) % 16
-        greet((x * 4 + yl * 2 + j // 8, j % 8))
-    greet(xp)
-    greet(xm)
+    for to in (partner, pair, xp, xm, zp, zm):
+        greet(to)
     for step in (1, 3):
         for c_ in range(2):
             greet(chip_y(step, c_))
-    pl.semaphore_wait(barrier, 21)
+    pl.semaphore_wait(barrier, 10)
 
     for i, w in enumerate(weights):
         send(wcols(w, c), wslot_one(i, d), wsend.at[0, 0], wrecv.at[0, 2], chip_y(1, c)).start()
-        send(wcols(w, 1 - c), wslot_one(i, d), wsend.at[0, 1], wrecv.at[0, 3], chip_y(3, 1 - c)).start()
         send(wcols(w, 1 - c), wslot_one(i, d), wsend.at[0, 2], wrecv.at[0, 1], partner).start()
 
     def exchange(h):
@@ -114,6 +110,9 @@
     def _():
         exchange(0).start()
         exchange(1).start()
+
+    for i, w in enumerate(weights):
+        send(wcols(w, 1 - c), wslot_one(i, d), wsend.at[0, 1], wrecv.at[0, 3], chip_y(3, 1 - c)).start()
 
     own = [d, x * 4 + yl * 2 + (1 - c), x * 4 + (1 - yl) * 2 + c, x * 4 + (1 - yl) * 2 + (1 - c)]
 
@@ -134,12 +133,26 @@
             send(wslot(e), wslot(e), wsend.at[2, k], wrecv.at[2, k], xm),
         )
 
+    def wpart(e, h):
+        return wbuf.at[:, pl.ds(pl.multiple_of(e * WR + h * (WR // 2), WR // 2), WR // 2), :]
+
     def x_second(k):
-        if k % 2 == 0:
-            e = shift(own[k], 3)
+        if k == 0:
+            e = shift(own[0], 3)
             return send(wslot(e), wslot(e), wsend.at[3, k], wrecv.at[3, k], xp)
-        e = shift(own[k], 1)
-        return send(wslot(e), wslot(e), wsend.at[3, k], wrecv.at[3, k], xm)
+        if k == 1:
+            e = shift(own[1], 1)
+            return send(wslot(e), wslot(e), wsend.at[3, k], wrecv.at[3, k], xm)
+        e = shift(own[2], 3 if k == 2 else 1)
+        return send(wpart(e, k - 2), wpart(e, k - 2), wsend.at[3, k], wrecv.at[3, k], xp if k == 2 else xm)
+
+    def y_second(k):
+        to = chip_y((1, 3)[k % 2], c)
+        if k < 2:
+            e = shift(own[1], (3, 1)[k])
+            return send(wslot(e), wslot(e), ysend.at[k], yrecv.at[k], to)
+        e = shift(own[1], 2)
+        return send(wpart(e, k - 2), wpart(e, k - 2), ysend.at[k], yrecv.at[k], to)
 
     def z_first(h):
         return (
@@ -180,11 +193,26 @@
         start_both(x_first(k))
 
     def x_forward(k):
-        if k % 2 == 0:
-            wait_w(1, k, shift(own[k], 3))
-        else:
-            wait_w(2, k, shift(own[k], 1))
+        wait_w(1 + k % 2, min(k, 2), shift(own[min(k, 2)], (3, 1)[k % 2]))
         x_second(k).start()
+
+    def y_forward(k):
+        if k == 0:
+            wait_w(1, 1, shift(own[1], 3))
+        if k == 2:
+            wait_w(3, 1, shift(own[1], 2))
+        y_second(k).start()
+
+    def wait_rest_w():
+        wait_w(2, 0, shift(own[0], 1))
+        wait_w(3, 0, shift(own[0], 2))
+        for h in range(2):
+            there = wpart(shift(own[2], 2), h)
+            send(there, there, wsend.at[0, 0], wrecv.at[3, 2 + h], partner).wait_recv()
+        wait_w(0, 3, own[3])
+        for k in range(4):
+            there = wslot(shift(own[3], (3, 1)[k])) if k < 2 else wpart(shift(own[3], 2), k - 2)
+            send(there, there, wsend.at[0, 0], yrecv.at[k], partner).wait_recv()
 
     def duty(role, g, h):
         @pl.when(role)
@@ -198,16 +226,16 @@
                     z_second(h).start()
             to_partner(g, h).start()
 
-    def ready(role, g):
+    def ready(role, g, halves=(0, 1)):
         @pl.when(role)
         def _():
-            for h in range(2):
+            for h in halves:
                 there = tbuf.at[(1 - c) * 4 + zs[g], pl.ds(h * HALF, HALF), :]
                 send(there, there, psend.at[g, h], precv.at[g, h], partner).wait_recv()
 
     gain_row = gain[...].astype(jnp.float32).reshape(1, D)
 
-    def norm(plane, g):
+    def norm(plane, g, halves=(0, 1)):
         block = plane * 4 + zs[g]
 
         def norm_rows(i, carry):
@@ -217,7 +245,8 @@
             nbuf[to, :] = (rows * scale * gain_row).astype(jnp.bfloat16)
             return carry
 
-        lax.fori_loop(0, ROWS // NCHUNK, norm_rows, 0)
+        per = HALF // NCHUNK
+        lax.fori_loop(halves[0] * per, (halves[-1] + 1) * per, norm_rows, 0, unroll=per)
 
     def turned(lin, rows):
         cosine, sine = cosb[rows, :], sinb[rows, :]
@@ -227,8 +256,8 @@
             parts.append((v * cosine + pltpu.roll(v, HD // 2, 1) * sine).astype(jnp.bfloat16))
         return parts
 
-    def project(first):
-        rows = pl.ds(pl.multiple_of(first * ROWS, ROWS), ROWS)
+    def project(first, blocks):
+        rows = pl.ds(pl.multiple_of(first * ROWS, ROWS), blocks * ROWS)
         block = nbuf[rows, :]
         q = jnp.dot(block, wbuf[0], preferred_element_type=jnp.float32)
         for h, part in enumerate(turned(q, rows)):
@@ -240,16 +269,6 @@
         for h in range(2):
             vbuf[h, rows, :] = v[:, h * HD : (h + 1) * HD]
 
-    def project_some(plane, groups):
-        lo, hi = groups
-
-        def one(g, carry):
-            z_ = lax.rem(z + jnp.where(g == 0, 0, jnp.where(g == 1, 3, jnp.where(g == 2, 1, 2))), 4)
-            project(plane * 4 + z_)
-            return carry
-
-        lax.fori_loop(lo, hi, one, 0)
-
     x_start(0)
     duty(home, 0, 0)
     duty(home, 0, 1)
@@ -257,50 +276,52 @@
     ready(away, 0)
     norm(yh, 0)
     x_start(2)
-    x_start(3)
-    duty(away, 0, 0)
     x_forward(0)
     duty(home, 1, 0)
+    duty(home, 2, 0)
+    duty(away, 0, 0)
     x_forward(1)
+    y_forward(0)
+    y_forward(1)
     duty(home, 2, 1)
     duty(home, 1, 1)
-    duty(home, 2, 0)
     duty(away, 0, 1)
     ready(away, 1)
     norm(yh, 1)
     x_forward(2)
+    x_forward(3)
     ready(away, 2)
     norm(yh, 2)
-    x_forward(3)
+    ready(home, 0)
+    norm(1 - yh, 0)
+    y_forward(2)
+    y_forward(3)
+    duty(away, 1, 0)
+    duty(away, 2, 0)
     duty(home, 3, 0)
     duty(home, 3, 1)
-    ready(home, 0)
-    norm(1 - yh, 0)
     ready(away, 3)
     norm(yh, 3)
-    duty(away, 1, 0)
+    wait_rest_w()
+    pltpu.make_async_copy(cos_hbm, cosb, lsem.at[0]).wait()
+    pltpu.make_async_copy(sin_hbm, sinb, lsem.at[1]).wait()
+    project(yh * 4, 2)
     duty(away, 2, 1)
     duty(away, 1, 1)
-    duty(away, 2, 0)
+    project(yh * 4 + 2, 2)
     ready(home, 1)
     norm(1 - yh, 1)
     ready(home, 2)
     norm(1 - yh, 2)
-    for k in (1, 3):
-        wait_w(1, k, shift(own[k], 3))
-    for k in (0, 2):
-        wait_w(2, k, shift(own[k], 1))
-    for k in range(4):
-        wait_w(3, k, shift(own[k], 2))
-    pltpu.make_async_copy(cos_hbm, cosb, lsem.at[0]).wait()
-    pltpu.make_async_copy(sin_hbm, sinb, lsem.at[1]).wait()
-    project_some(yh, (0, 4))
+    project((1 - yh) * 4 + z - z % 2, 2)
     duty(away, 3, 0)
+    project((1 - yh) * 4 + (z + jnp.where(z % 2 == 0, 3, 1)) % 4, 1)
+    ready(home, 3, (0,))
+    norm(1 - yh, 3, (0,))
     duty(away, 3, 1)
-    project_some(1 - yh, (0, 3))
-    ready(home, 3)
-    norm(1 - yh, 3)
-    project_some(1 - yh, (3, 4))
+    ready(home, 3, (1,))
+    norm(1 - yh, 3, (1,))
+    project((1 - yh) * 4 + zs[3], 1)
 
     factor = HD ** (-0.5) * math.log2(math.e)
     nt = (((1,), (1,)), ((), ()))
@@ -344,7 +365,7 @@
             obuf[pl.ds(j * QB, QB), pl.ds(pl.multiple_of(h * HD, HD), HD)] = (acc / total).astype(jnp.bfloat16)
             return carry
 
-        lax.fori_loop(0, 2, one_head, 0)
+        lax.fori_loop(0, 2, one_head, 0, unroll=True)
         while sent < 8 and (sent + 1) * ROWS <= (j + 1) * QB:
 
             @pl.when(own_block(sent))
@@ -379,9 +400,11 @@
     for i in range(3):
         send(wslot(d), wslot(d), wsend.at[0, i], wrecv.at[0, 0], partner).wait_send()
     for k in range(4):
-        for copy in x_first(k):
-            copy.wait_send()
+        if k < 3:
+            for copy in x_first(k):
+                copy.wait_send()
         x_second(k).wait_send()
+        y_second(k).wait_send()
     for h in range(2):
 
         @pl.when(away)
@@ -414,6 +437,8 @@
             pltpu.VMEM((LEN, WC), bf),
             pltpu.VMEM((LEN, HD), jnp.float32),
             pltpu.VMEM((LEN, HD), jnp.float32),
+            dma((4,)),
+            dma((4,)),
             dma((4, 4)),
             dma((4, 4)),
             dma((4, 2)),

time: 70.4 us -> 64.6 us (0.918)
  the two profiles are of different devices: /device:TPU:112 before, /device:TPU:17 now
where the time goes in v3:
time: 64.6 us; the launch traced here: 64.4 us
  Pallas kernels  62.2 us (96%)
  local copies, waits for them, and re-layouts  2.2 us (3%)
    pallas_call x1, Pallas kernels, shards(): pl.pallas_call(kernel, out_shape=jax.ShapeDtypeStruct((ROWS, D), bf), in_...  62.2 us
    unnamed x1, local copies, waits for them, and re-layouts  2.2 us

profile of v3, /device:TPU:17, one launch (start us, length us, event | category | flops | bytes accessed | tf_op | source)
XLA Modules:
  0.0 64.4 jit_solution(9850048901435169117)
XLA Ops:
  0.0 62.2 %attention_block.1 = bf16[224,2048]{1,0:T(8,128)(2,1)} custom-call(bf16[224,2048]{1,0:T(8,128)(2,1)} %bitcast.3, bf16[2048]{0:T(1024)(128)(2,1)} %gain.1, bf16[128,2048]{1,0:T(8,128)(2,1)} %qw.1, bf16[128,2048]{1,0:T(8,128)(2,1)} %kw.1, bf16[128,2048]{1,0:T(8,128)(2,1)} %vw.1, f32[1792,128]{1,0:T(8,128)} %constant.4.clone.cos_hbm, ...), custom_call_target="tpu_custom_call" | custom-call | tf_op jit(solution)/shard_map/attention_block/pallas_call | solution.py:425
  62.2 2.2 %copy.9 = bf16[1,224,2048]{2,1,0:T(8,128)(2,1)} copy(bf16[1,224,2048]{2,1,0:T(8,128)(2,1)} %bitcast.2) | data formatting | bytes 1835008

commit v4 on v3

--- a/solution.py
+++ b/solution.py
@@ -17,9 +17,9 @@
 LEN = 1792
 WR = 128
 WC = 256
-HALF = ROWS // 2
 QB = 256
 NQ = LEN // QB
+PIECES = ((0, 64), (64, 48), (112, 64), (176, 48))
 NCHUNK = 16
 
 
@@ -35,7 +35,7 @@
 
 def kernel(
     tok, gain, qw, kw, vw, cos_hbm, sin_hbm, out,
-    tbuf, nbuf, wbuf, qbuf, kbuf, vbuf, obuf, cosb, sinb,
+    tbuf, nbuf, wbuf, lin, qbuf, kbuf, vbuf, obuf, cosb, sinb,
     yrecv, ysend, wrecv, wsend, trecv, tsend, precv, psend, osend, orecv, lsem,
 ):
     d, t = lax.axis_index("dp"), lax.axis_index("ctx")
@@ -71,8 +71,11 @@
     def wcols(ref, c_):
         return ref.at[:, pl.ds(pl.multiple_of(z * 512 + c_ * WC, WC), WC)]
 
+    def rows_of(i):
+        return pl.ds(*PIECES[i])
+
     def tslot(z_, h):
-        return tbuf.at[c * 4 + z_, pl.ds(h * HALF, HALF), :]
+        return tbuf.at[c * 4 + z_, rows_of(h), :]
 
     weights = (qw, kw, vw)
     for i, w in enumerate(weights):
@@ -80,8 +83,8 @@
 
     @pl.when(home)
     def _():
-        for h in range(2):
-            pltpu.make_async_copy(tok.at[pl.ds(h * HALF, HALF), :], tslot(z, h), trecv.at[0, h]).start()
+        for h in range(4):
+            pltpu.make_async_copy(tok.at[rows_of(h), :], tslot(z, h), trecv.at[0, h]).start()
 
     pltpu.make_async_copy(cos_hbm, cosb, lsem.at[0]).start()
     pltpu.make_async_copy(sin_hbm, sinb, lsem.at[1]).start()
@@ -103,13 +106,13 @@
         send(wcols(w, 1 - c), wslot_one(i, d), wsend.at[0, 2], wrecv.at[0, 1], partner).start()
 
     def exchange(h):
-        there = tbuf.at[(1 - c) * 4 + z, pl.ds(h * HALF, HALF), :]
-        return send(tok.at[pl.ds(h * HALF, HALF), :], there, tsend.at[0, h], trecv.at[0, h], pair)
+        there = tbuf.at[(1 - c) * 4 + z, rows_of(h), :]
+        return send(tok.at[rows_of(h), :], there, tsend.at[0, h], trecv.at[0, h], pair)
 
     @pl.when(away)
     def _():
-        exchange(0).start()
-        exchange(1).start()
+        for h in (0, 2, 1, 3):
+            exchange(h).start()
 
     for i, w in enumerate(weights):
         send(wcols(w, 1 - c), wslot_one(i, d), wsend.at[0, 1], wrecv.at[0, 3], chip_y(3, 1 - c)).start()
@@ -161,8 +164,8 @@
         )
 
     def z_second(h):
-        z_ = (z + (3, 1)[h]) % 4
-        return send(tslot(z_, h), tslot(z_, h), tsend.at[3, h], trecv.at[3, h], (zp, zm)[h])
+        z_ = (z + (3, 1)[h // 2]) % 4
+        return send(tslot(z_, h), tslot(z_, h), tsend.at[3, h], trecv.at[3, h], (zp, zm)[h // 2])
 
     zs = [z, (z + 3) % 4, (z + 1) % 4, (z + 2) % 4]
 
@@ -175,7 +178,7 @@
     def wait_own_t(h):
         @pl.when(home)
         def _():
-            pltpu.make_async_copy(tok.at[pl.ds(h * HALF, HALF), :], tslot(z, h), trecv.at[0, h]).wait()
+            pltpu.make_async_copy(tok.at[rows_of(h), :], tslot(z, h), trecv.at[0, h]).wait()
 
         @pl.when(away)
         def _():
@@ -203,39 +206,51 @@
             wait_w(3, 1, shift(own[1], 2))
         y_second(k).start()
 
-    def wait_rest_w():
+    def wait_y(k):
+        there = wslot(shift(own[3], (3, 1)[k])) if k < 2 else wpart(shift(own[3], 2), k - 2)
+        send(there, there, wsend.at[0, 0], yrecv.at[k], partner).wait_recv()
+
+    def wait_nearby_w():
         wait_w(2, 0, shift(own[0], 1))
+        wait_w(0, 3, own[3])
+        wait_y(0)
+        wait_y(1)
+
+    def wait_across_w():
         wait_w(3, 0, shift(own[0], 2))
         for h in range(2):
             there = wpart(shift(own[2], 2), h)
             send(there, there, wsend.at[0, 0], wrecv.at[3, 2 + h], partner).wait_recv()
-        wait_w(0, 3, own[3])
-        for k in range(4):
-            there = wslot(shift(own[3], (3, 1)[k])) if k < 2 else wpart(shift(own[3], 2), k - 2)
-            send(there, there, wsend.at[0, 0], yrecv.at[k], partner).wait_recv()
+        wait_y(2)
+        wait_y(3)
 
     def duty(role, g, h):
         @pl.when(role)
         def _():
             if g == 0:
                 wait_own_t(h)
-                start_both(z_first(h))
+                z_first(h)[h // 2].start()
+                if h == 3:
+                    z_first(2)[0].start()
+                    z_first(0)[1].start()
+                    z_first(3)[0].start()
+                    z_first(1)[1].start()
             else:
                 wait_t(g, h)
-                if (g, h) in ((1, 0), (2, 1)):
+                if (g, h // 2) in ((1, 0), (2, 1)):
                     z_second(h).start()
             to_partner(g, h).start()
 
-    def ready(role, g, halves=(0, 1)):
+    def ready(role, g, pieces=(0, 1, 2, 3)):
         @pl.when(role)
         def _():
-            for h in halves:
-                there = tbuf.at[(1 - c) * 4 + zs[g], pl.ds(h * HALF, HALF), :]
+            for h in pieces:
+                there = tbuf.at[(1 - c) * 4 + zs[g], rows_of(h), :]
                 send(there, there, psend.at[g, h], precv.at[g, h], partner).wait_recv()
 
     gain_row = gain[...].astype(jnp.float32).reshape(1, D)
 
-    def norm(plane, g, halves=(0, 1)):
+    def norm(plane, g, pieces=(0, 3)):
         block = plane * 4 + zs[g]
 
         def norm_rows(i, carry):
@@ -245,82 +260,111 @@
             nbuf[to, :] = (rows * scale * gain_row).astype(jnp.bfloat16)
             return carry
 
-        per = HALF // NCHUNK
-        lax.fori_loop(halves[0] * per, (halves[-1] + 1) * per, norm_rows, 0, unroll=per)
-
-    def turned(lin, rows):
+        lo, hi = PIECES[pieces[0]][0] // NCHUNK, sum(PIECES[pieces[1]]) // NCHUNK
+        lax.fori_loop(lo, hi, norm_rows, 0, unroll=7)
+
+    def turned(product, rows):
         cosine, sine = cosb[rows, :], sinb[rows, :]
         parts = []
         for h in range(2):
-            v = lin[:, h * HD : (h + 1) * HD]
+            v = product[:, h * HD : (h + 1) * HD]
             parts.append((v * cosine + pltpu.roll(v, HD // 2, 1) * sine).astype(jnp.bfloat16))
         return parts
 
-    def project(first, blocks):
+    def dots(rows, i, chips):
+        total = None
+        for x_ in chips:
+            depth = pl.ds(pl.multiple_of(x_ * 4 * WR, 4 * WR), 4 * WR)
+            part = jnp.dot(nbuf[rows, depth], wbuf[i, depth, :], preferred_element_type=jnp.float32)
+            total = part if total is None else total + part
+        return total
+
+    nearby, across = (x, (x + 3) % 4, (x + 1) % 4), (x + 2) % 4
+
+    def project_nearby(first, local):
+        rows = pl.ds(pl.multiple_of(first * ROWS, ROWS), 2 * ROWS)
+        for i in range(3):
+            lin[i, pl.ds(local * ROWS, 2 * ROWS), :] = dots(rows, i, nearby)
+
+    def project(first, blocks, local=None):
         rows = pl.ds(pl.multiple_of(first * ROWS, ROWS), blocks * ROWS)
-        block = nbuf[rows, :]
-        q = jnp.dot(block, wbuf[0], preferred_element_type=jnp.float32)
-        for h, part in enumerate(turned(q, rows)):
-            qbuf[h, rows, :] = part
-        k = jnp.dot(block, wbuf[1], preferred_element_type=jnp.float32)
-        for h, part in enumerate(turned(k, rows)):
-            kbuf[h, rows, :] = part
-        v = jnp.dot(block, wbuf[2], preferred_element_type=jnp.float32).astype(jnp.bfloat16)
+
+        def product(i):
+            if local is None:
+                return jnp.dot(nbuf[rows, :], wbuf[i], preferred_element_type=jnp.float32)
+            return lin[i, pl.ds(local * ROWS, blocks * ROWS), :] + dots(rows, i, (across,))
+
+        for buf, i in ((qbuf, 0), (kbuf, 1)):
+            for h, part in enumerate(turned(product(i), rows)):
+                buf[h, rows, :] = part
+        v = product(2).astype(jnp.bfloat16)
         for h in range(2):
             vbuf[h, rows, :] = v[:, h * HD : (h + 1) * HD]
 
+    def duties(role, g, pieces):
+        for h in pieces:
+            duty(role, g, h)
+
     x_start(0)
-    duty(home, 0, 0)
-    duty(home, 0, 1)
+    duties(home, 0, (0, 2, 1, 3))
     x_start(1)
     ready(away, 0)
     norm(yh, 0)
+    duty(home, 1, 0)
+    duty(home, 2, 2)
     x_start(2)
     x_forward(0)
-    duty(home, 1, 0)
-    duty(home, 2, 0)
-    duty(away, 0, 0)
+    duty(home, 1, 1)
+    duty(home, 2, 3)
     x_forward(1)
     y_forward(0)
     y_forward(1)
-    duty(home, 2, 1)
-    duty(home, 1, 1)
-    duty(away, 0, 1)
+    duty(away, 0, 0)
+    duty(away, 0, 2)
+    duties(home, 2, (0, 1))
+    duties(home, 1, (2, 3))
+    x_forward(2)
+    x_forward(3)
+    duties(away, 0, (1, 3))
     ready(away, 1)
     norm(yh, 1)
-    x_forward(2)
-    x_forward(3)
     ready(away, 2)
     norm(yh, 2)
+    duty(away, 1, 0)
+    duty(away, 2, 2)
+    y_forward(2)
+    y_forward(3)
+    duties(home, 3, (0, 2, 1, 3))
     ready(home, 0)
     norm(1 - yh, 0)
-    y_forward(2)
-    y_forward(3)
-    duty(away, 1, 0)
-    duty(away, 2, 0)
-    duty(home, 3, 0)
-    duty(home, 3, 1)
     ready(away, 3)
     norm(yh, 3)
-    wait_rest_w()
+    duty(away, 1, 1)
+    duty(away, 2, 3)
+    wait_nearby_w()
     pltpu.make_async_copy(cos_hbm, cosb, lsem.at[0]).wait()
     pltpu.make_async_copy(sin_hbm, sinb, lsem.at[1]).wait()
-    project(yh * 4, 2)
-    duty(away, 2, 1)
-    duty(away, 1, 1)
-    project(yh * 4 + 2, 2)
+    project_nearby(yh * 4, 0)
+    project_nearby(yh * 4 + 2, 2)
+    wait_across_w()
+    project(yh * 4, 2, 0)
+    duties(away, 1, (2, 3))
+    duties(away, 2, (0, 1))
+    project(yh * 4 + 2, 2, 2)
     ready(home, 1)
     norm(1 - yh, 1)
     ready(home, 2)
     norm(1 - yh, 2)
     project((1 - yh) * 4 + z - z % 2, 2)
     duty(away, 3, 0)
+    duty(away, 3, 2)
     project((1 - yh) * 4 + (z + jnp.where(z % 2 == 0, 3, 1)) % 4, 1)
-    ready(home, 3, (0,))
-    norm(1 - yh, 3, (0,))
     duty(away, 3, 1)
-    ready(home, 3, (1,))
-    norm(1 - yh, 3, (1,))
+    ready(home, 3, (0, 1))
+    norm(1 - yh, 3, (0, 1))
+    duty(away, 3, 3)
+    ready(home, 3, (2, 3))
+    norm(1 - yh, 3, (2, 3))
     project((1 - yh) * 4 + zs[3], 1)
 
     factor = HD ** (-0.5) * math.log2(math.e)
@@ -330,53 +374,67 @@
     allowed = cols_i <= rows_i
     mycols = pl.ds(pl.multiple_of(z * 512 + c * WC, WC), WC)
 
-    def to_owner(b):
+    def parts(j):
+        found = []
+        for b in range(8):
+            lo, hi = max(b * ROWS, j * QB), min((b + 1) * ROWS, (j + 1) * QB)
+            if lo < hi:
+                found.append((b, lo - b * ROWS, lo, hi - lo))
+        return found
+
+    def to_owner(b, first, row, n):
         return send(
-            obuf.at[pl.ds(b * ROWS, ROWS), :], out.at[:, mycols], osend.at[b], orecv.at[z * 2 + c],
+            obuf.at[pl.ds(row, n), :], out.at[pl.ds(first, n), mycols], osend.at[b], orecv.at[z * 2 + c],
             dev(x, yl, yh, b // 4, b % 4),
         )
 
-    def to_self(b):
-        return pltpu.make_async_copy(obuf.at[pl.ds(b * ROWS, ROWS), :], out.at[:, mycols], osend.at[b])
+    def to_self(b, first, row, n):
+        return pltpu.make_async_copy(obuf.at[pl.ds(row, n), :], out.at[pl.ds(first, n), mycols], osend.at[b])
 
     def own_block(b):
         return jnp.logical_and(home, t == b)
 
-    sent = 0
-    for j in range(NQ):
-
-        def one_head(h, carry, j=j):
-            q = qbuf[h, pl.ds(j * QB, QB), :]
-            s_d = lax.dot_general(q, kbuf[h, pl.ds(j * QB, QB), :], nt, preferred_element_type=jnp.float32)
-            s_d = jnp.where(allowed, s_d, -1e30)
-            top = jnp.max(s_d, axis=1, keepdims=True)
-            if j:
-                s_p = lax.dot_general(q, kbuf[h, pl.ds(0, j * QB), :], nt, preferred_element_type=jnp.float32)
-                top = jnp.maximum(top, jnp.max(s_p, axis=1, keepdims=True))
-            e_d = jnp.exp2((s_d - top) * factor)
-            total = jnp.sum(e_d, axis=1, keepdims=True)
-            acc = jnp.dot(e_d.astype(jnp.bfloat16), vbuf[h, pl.ds(j * QB, QB), :], preferred_element_type=jnp.float32)
-            if j:
-                e_p = jnp.exp2((s_p - top) * factor)
-                total = total + jnp.sum(e_p, axis=1, keepdims=True)
-                acc = acc + jnp.dot(
-                    e_p.astype(jnp.bfloat16), vbuf[h, pl.ds(0, j * QB), :], preferred_element_type=jnp.float32
-                )
-            obuf[pl.ds(j * QB, QB), pl.ds(pl.multiple_of(h * HD, HD), HD)] = (acc / total).astype(jnp.bfloat16)
-            return carry
-
-        lax.fori_loop(0, 2, one_head, 0, unroll=True)
-        while sent < 8 and (sent + 1) * ROWS <= (j + 1) * QB:
-
-            @pl.when(own_block(sent))
-            def _(b=sent):
-                to_self(b).start()
-
-            @pl.when(jnp.logical_not(own_block(sent)))
-            def _(b=sent):
-                to_owner(b).start()
-
-            sent += 1
+    def attend(b, h):
+        rows, past = pl.ds(b * QB, QB), pl.ds(0, b * QB)
+        q = qbuf[h, rows, :]
+        s_d = lax.dot_general(q, kbuf[h, rows, :], nt, preferred_element_type=jnp.float32)
+        s_d = jnp.where(allowed, s_d, -1e30)
+        top = jnp.max(s_d, axis=1, keepdims=True)
+        if b:
+            s_p = lax.dot_general(q, kbuf[h, past, :], nt, preferred_element_type=jnp.float32)
+            top = jnp.maximum(top, jnp.max(s_p, axis=1, keepdims=True))
+        e_d = jnp.exp2((s_d - top) * factor)
+        total = jnp.sum(e_d, axis=1, keepdims=True)
+        acc = jnp.dot(e_d.astype(jnp.bfloat16), vbuf[h, rows, :], preferred_element_type=jnp.float32)
+        if b:
+            e_p = jnp.exp2((s_p - top) * factor)
+            total = total + jnp.sum(e_p, axis=1, keepdims=True)
+            acc = acc + jnp.dot(e_p.astype(jnp.bfloat16), vbuf[h, past, :], preferred_element_type=jnp.float32)
+        obuf[rows, h * HD : (h + 1) * HD] = (acc / total).astype(jnp.bfloat16)
+
+    def one_block(i, carry):
+        far = (z + 2) % 4
+        near = far - jnp.where(far > 1, 1, 0)
+        j_ = jnp.where(i < 4, (1 - yh) * 3 + (far + i) % 4, yh * 4 + (near + i - 4) % 3)
+        for j in range(NQ):
+
+            @pl.when(j_ == j)
+            def _(j=j):
+                for h in range(2):
+                    attend(j, h)
+                for part in parts(j):
+
+                    @pl.when(own_block(part[0]))
+                    def _(part=part):
+                        to_self(*part).start()
+
+                    @pl.when(jnp.logical_not(own_block(part[0])))
+                    def _(part=part):
+                        to_owner(*part).start()
+
+        return carry
+
+    lax.fori_loop(0, NQ, one_block, 0)
 
     for z_ in range(4):
         for c_ in range(2):
@@ -391,11 +449,11 @@
 
         @pl.when(own_block(b))
         def _(b=b):
-            to_self(b).wait()
+            to_self(b, 0, b * ROWS, ROWS).wait()
 
         @pl.when(jnp.logical_not(own_block(b)))
         def _(b=b):
-            to_owner(b).wait_send()
+            to_owner(b, 0, b * ROWS, ROWS).wait_send()
 
     for i in range(3):
         send(wslot(d), wslot(d), wsend.at[0, i], wrecv.at[0, 0], partner).wait_send()
@@ -405,7 +463,7 @@
                 copy.wait_send()
         x_second(k).wait_send()
         y_second(k).wait_send()
-    for h in range(2):
+    for h in range(4):
 
         @pl.when(away)
         def _(h=h):
@@ -431,6 +489,7 @@
             pltpu.VMEM((8, ROWS, D), bf),
             pltpu.VMEM((LEN, D), bf),
             pltpu.VMEM((3, D, WC), bf),
+            pltpu.VMEM((3, 4 * ROWS, WC), jnp.float32),
             pltpu.VMEM((2, LEN, HD), bf),
             pltpu.VMEM((2, LEN, HD), bf),
             pltpu.VMEM((2, LEN, HD), bf),
@@ -441,10 +500,10 @@
             dma((4,)),
             dma((4, 4)),
             dma((4, 4)),
-            dma((4, 2)),
-            dma((4, 2)),
-            dma((4, 2)),
-            dma((4, 2)),
+            dma((4, 4)),
+            dma((4, 4)),
+            dma((4, 4)),
+            dma((4, 4)),
             dma((8,)),
             dma((8,)),
             dma((2,)),

time: 64.6 us -> 62 us (0.960)
  the two profiles are of different devices: /device:TPU:17 before, /device:TPU:0 now
where the time goes in v4:
time: 62 us; the launch traced here: 61.8 us
  Pallas kernels  59.6 us (96%)
  local copies, waits for them, and re-layouts  2.2 us (4%)
    pallas_call x1, Pallas kernels, shards(): pl.pallas_call(kernel, out_shape=jax.ShapeDtypeStruct((ROWS, D), bf), in_...  59.6 us
    unnamed x1, local copies, waits for them, and re-layouts  2.2 us

profile of v4, /device:TPU:0, one launch (start us, length us, event | category | flops | bytes accessed | tf_op | source)
XLA Modules:
  0.0 61.8 jit_solution(5115482321969830274)
XLA Ops:
  0.0 59.6 %attention_block.1 = bf16[224,2048]{1,0:T(8,128)(2,1)} custom-call(bf16[224,2048]{1,0:T(8,128)(2,1)} %bitcast.3, bf16[2048]{0:T(1024)(128)(2,1)} %gain.1, bf16[128,2048]{1,0:T(8,128)(2,1)} %qw.1, bf16[128,2048]{1,0:T(8,128)(2,1)} %kw.1, bf16[128,2048]{1,0:T(8,128)(2,1)} %vw.1, f32[1792,128]{1,0:T(8,128)} %constant.4.clone.cos_hbm, ...), custom_call_target="tpu_custom_call" | custom-call | tf_op jit(solution)/shard_map/attention_block/pallas_call | solution.py:483
  59.6 2.2 %copy.9 = bf16[1,224,2048]{2,1,0:T(8,128)(2,1)} copy(bf16[1,224,2048]{2,1,0:T(8,128)(2,1)} %bitcast.2) | data formatting | bytes 1835008

commit v5 on v4

--- a/solution.py
+++ b/solution.py
@@ -413,9 +413,11 @@
         obuf[rows, h * HD : (h + 1) * HD] = (acc / total).astype(jnp.bfloat16)
 
     def one_block(i, carry):
-        far = (z + 2) % 4
-        near = far - jnp.where(far > 1, 1, 0)
-        j_ = jnp.where(i < 4, (1 - yh) * 3 + (far + i) % 4, yh * 4 + (near + i - 4) % 3)
+        first = (z + 1) % 4
+        near = first - jnp.where(first > 1, 1, 0)
+        early = jnp.where(i < 3, (near + i) % 3, 3 + (first + i - 3) % 4)
+        late = jnp.where(i < 4, (first + i) % 4, 4 + (near + i - 4) % 3)
+        j_ = jnp.where(yh == 0, early, late)
         for j in range(NQ):
 
             @pl.when(j_ == j)

time: 62 us -> 61.2 us (0.987)
  the two profiles are of different devices: /device:TPU:0 before, /device:TPU:17 now
where the time goes in v5:
time: 61.2 us; the launch traced here: 60.9 us
  Pallas kernels  58.7 us (96%)
  local copies, waits for them, and re-layouts  2.2 us (4%)
    pallas_call x1, Pallas kernels, shards(): pl.pallas_call(kernel, out_shape=jax.ShapeDtypeStruct((ROWS, D), bf), in_...  58.7 us
    unnamed x1, local copies, waits for them, and re-layouts  2.2 us

profile of v5, /device:TPU:17, one launch (start us, length us, event | category | flops | bytes accessed | tf_op | source)
XLA Modules:
  0.0 60.9 jit_solution(8512234272462590490)
XLA Ops:
  0.0 58.7 %attention_block.1 = bf16[224,2048]{1,0:T(8,128)(2,1)} custom-call(bf16[224,2048]{1,0:T(8,128)(2,1)} %bitcast.3, bf16[2048]{0:T(1024)(128)(2,1)} %gain.1, bf16[128,2048]{1,0:T(8,128)(2,1)} %qw.1, bf16[128,2048]{1,0:T(8,128)(2,1)} %kw.1, bf16[128,2048]{1,0:T(8,128)(2,1)} %vw.1, f32[1792,128]{1,0:T(8,128)} %constant.4.clone.cos_hbm, ...), custom_call_target="tpu_custom_call" | custom-call | tf_op jit(solution)/shard_map/attention_block/pallas_call | solution.py:485
  58.7 2.2 %copy.9 = bf16[1,224,2048]{2,1,0:T(8,128)(2,1)} copy(bf16[1,224,2048]{2,1,0:T(8,128)(2,1)} %bitcast.2) | data formatting | bytes 1835008

commit v6 on v5

--- a/solution.py
+++ b/solution.py
@@ -394,23 +394,27 @@
     def own_block(b):
         return jnp.logical_and(home, t == b)
 
-    def attend(b, h):
+    def attend(b):
         rows, past = pl.ds(b * QB, QB), pl.ds(0, b * QB)
-        q = qbuf[h, rows, :]
-        s_d = lax.dot_general(q, kbuf[h, rows, :], nt, preferred_element_type=jnp.float32)
-        s_d = jnp.where(allowed, s_d, -1e30)
-        top = jnp.max(s_d, axis=1, keepdims=True)
-        if b:
-            s_p = lax.dot_general(q, kbuf[h, past, :], nt, preferred_element_type=jnp.float32)
-            top = jnp.maximum(top, jnp.max(s_p, axis=1, keepdims=True))
-        e_d = jnp.exp2((s_d - top) * factor)
-        total = jnp.sum(e_d, axis=1, keepdims=True)
-        acc = jnp.dot(e_d.astype(jnp.bfloat16), vbuf[h, rows, :], preferred_element_type=jnp.float32)
-        if b:
-            e_p = jnp.exp2((s_p - top) * factor)
-            total = total + jnp.sum(e_p, axis=1, keepdims=True)
-            acc = acc + jnp.dot(e_p.astype(jnp.bfloat16), vbuf[h, past, :], preferred_element_type=jnp.float32)
-        obuf[rows, h * HD : (h + 1) * HD] = (acc / total).astype(jnp.bfloat16)
+        both, spans = range(2), (rows, past) if b else (rows,)
+        scores = [
+            [
+                lax.dot_general(qbuf[h, rows, :], kbuf[h, span, :], nt, preferred_element_type=jnp.float32)
+                for span in spans
+            ]
+            for h in both
+        ]
+        for h in both:
+            scores[h][0] = jnp.where(allowed, scores[h][0], -1e30)
+        top = [functools.reduce(jnp.maximum, [jnp.max(p, axis=1, keepdims=True) for p in scores[h]]) for h in both]
+        expo = [[jnp.exp2((p - top[h]) * factor) for p in scores[h]] for h in both]
+        total = [sum(jnp.sum(p, axis=1, keepdims=True) for p in expo[h]) for h in both]
+        for h in both:
+            acc = sum(
+                jnp.dot(p.astype(jnp.bfloat16), vbuf[h, span, :], preferred_element_type=jnp.float32)
+                for p, span in zip(expo[h], spans)
+            )
+            obuf[rows, h * HD : (h + 1) * HD] = (acc / total[h]).astype(jnp.bfloat16)
 
     def one_block(i, carry):
         first = (z + 1) % 4
@@ -422,8 +426,7 @@
 
             @pl.when(j_ == j)
             def _(j=j):
-                for h in range(2):
-                    attend(j, h)
+                attend(j)
                 for part in parts(j):
 
                     @pl.when(own_block(part[0]))

time: 61.2 us -> 60 us (0.980)
  Pallas kernels: 58.7 us -> 57.4 us
    pallas_call x1, Pallas kernels: 58.7 us -> 57.4 us  [shards(): pl.pallas_call(kernel, out_shape=jax.ShapeDtypeStruct((ROWS, D), bf), in_...]
where the time goes in v6:
time: 60 us; the launch traced here: 59.6 us
  Pallas kernels  57.4 us (96%)
  local copies, waits for them, and re-layouts  2.2 us (4%)
    pallas_call x1, Pallas kernels, shards(): pl.pallas_call(kernel, out_shape=jax.ShapeDtypeStruct((ROWS, D), bf), in_...  57.4 us
    unnamed x1, local copies, waits for them, and re-layouts  2.2 us

profile of v6, /device:TPU:17, one launch (start us, length us, event | category | flops | bytes accessed | tf_op | source)
XLA Modules:
  0.0 59.6 jit_solution(5756931234397540335)
XLA Ops:
  0.0 57.4 %attention_block.1 = bf16[224,2048]{1,0:T(8,128)(2,1)} custom-call(bf16[224,2048]{1,0:T(8,128)(2,1)} %bitcast.3, bf16[2048]{0:T(1024)(128)(2,1)} %gain.1, bf16[128,2048]{1,0:T(8,128)(2,1)} %qw.1, bf16[128,2048]{1,0:T(8,128)(2,1)} %kw.1, bf16[128,2048]{1,0:T(8,128)(2,1)} %vw.1, f32[1792,128]{1,0:T(8,128)} %constant.4.clone.cos_hbm, ...), custom_call_target="tpu_custom_call" | custom-call | tf_op jit(solution)/shard_map/attention_block/pallas_call | solution.py:488
  57.5 2.2 %copy.9 = bf16[1,224,2048]{2,1,0:T(8,128)(2,1)} copy(bf16[1,224,2048]{2,1,0:T(8,128)(2,1)} %bitcast.2) | data formatting | bytes 1835008
